TPU v7x, 32 devices: a whole 2x2x4 slice. The times are simulated.
32 devices in a mesh: dp: 2 (over y), ctx: 8 (over z, x), segment: 2 (over core).
Axes of the slice: x: 2, y: 2, z: 4, core: 2. Of those that a mesh axis runs over, the one named last changes fastest.
Arguments:
- inputs: bfloat16 [2, 2048, 1536], P('dp', 'ctx'), may hold values from -6 to 6
- cotangent: bfloat16 [2, 2048, 1536], P('dp', 'ctx'), may hold values from -6 to 6
- weights: bfloat16 [2, 1536, 1536], P('segment', 'ctx'), may hold values from -0.15625 to 0.15625
- tap_weights: float32 [2, 3, 1536], P('segment'), may hold values from -3 to 3
- projection: bfloat16 [2, 1536, 256], P('segment'), may hold values from -0.15625 to 0.15625
- dilations: int32 [2], replicated, may hold values from 1 to 64, as said below
Outputs:
- input_grad: bfloat16 [2, 2048, 1536], P('dp', 'ctx', 'segment')
- sketches: float32 [2, 256, 1536], P('segment', 'ctx')
Inputs may be any that keep to these rules, and one draw needn't show every extreme that they name: `dilations`: each entry is a section's dilation; one of the two equals 64.
All inputs are finite; a program needn't handle non-finite values.
Results may differ from a plain program's by a relative error of at most 0.02.
Values may be sent and summed in bfloat16 or wider, within the bound.
A program may use at most 64 MiB of HBM per device.

v0:
```python
import jax
import jax.numpy as jnp
from jax import lax
from jax.sharding import PartitionSpec as P

DMAX = 64


def with_halo(x, sides, width):
    for axis, dim in sides:
        devices, length = (lax.axis_size(axis), x.shape[dim])
        up = [(i, (i + 1) % devices) for i in range(devices - 1)]
        down = [(j, i) for i, j in up]
        last = lax.slice_in_dim(x, length - width, length, axis=dim)
        leading = lax.slice_in_dim(x, 0, width, axis=dim)
        before = lax.ppermute(last, axis, up)
        after = lax.ppermute(leading, axis, down)
        x = jnp.concatenate([before, x, after], axis=dim)
    return x


def passed_along(block, axis, distance):
    devices = range(lax.axis_size(axis))
    route = [(i - distance, i) for i in devices if i - distance in devices]
    return lax.ppermute(block, axis, route)


def activate(values):
    normed = values * lax.rsqrt(jnp.mean(values * values, axis=-1, keepdims=True) + 1e-06)
    return jax.nn.gelu(normed, approximate=True)


def shards(inputs, cotangent, weights, tap_weights, projection, dilations):
    segment_index = lax.axis_index("segment")
    width = inputs.shape[2]
    pair_weights, pair_taps, pair_tests = (weights, tap_weights, projection)
    rows_in = inputs[0]
    grad_out = cotangent[0]
    own_dilation = jnp.where(segment_index == 0, dilations[0], dilations[1])
    late_index = 0
    length = rows_in.shape[0]

    def act_rims(values):
        return with_halo(values, (("ctx", 0),), DMAX)

    def grad_rims(values):
        return with_halo(values, (("ctx", 0),), DMAX)

    full_weights = lax.all_gather(pair_weights, "ctx", axis=1, tiled=True)

    def backward_product(grad, which):
        return lax.dot_general(
            grad, full_weights[which], (((1,), (1,)), ((), ())), preferred_element_type=jnp.float32
        )

    def mix(rows, which, dilation):
        taps = pair_taps[which]
        lower = DMAX - dilation
        upper = DMAX + dilation
        activated = activate(rows.astype(jnp.float32)).astype(jnp.bfloat16)
        padded = act_rims(activated)
        before = lax.dynamic_slice_in_dim(padded, lower, length, 0)
        after = lax.dynamic_slice_in_dim(padded, upper, length, 0)
        mixed = taps[0] * before + taps[1] * activated + taps[2] * after
        return mixed.astype(jnp.bfloat16)

    def backward(rows, mixed, grad, which, dilation):
        taps = pair_taps[which]
        lower = DMAX - dilation
        upper = DMAX + dilation
        grad_mixed = backward_product(grad, which).astype(jnp.bfloat16)
        padded = grad_rims(grad_mixed)
        ahead = lax.dynamic_slice_in_dim(padded, upper, length, 0)
        behind = lax.dynamic_slice_in_dim(padded, lower, length, 0)
        grad_act = taps[0] * ahead + taps[1] * grad_mixed + taps[2] * behind
        primal, pullback = jax.vjp(activate, rows.astype(jnp.float32))
        grad_rows = pullback(grad_act)[0]
        grad_in = (grad.astype(jnp.float32) + grad_rows).astype(jnp.bfloat16)
        sketched = jnp.dot(grad, pair_tests[which], preferred_element_type=jnp.float32).astype(
            jnp.bfloat16
        )
        sketch = lax.dot_general(
            sketched, mixed, (((0,), (0,)), ((), ())), preferred_element_type=jnp.float32
        )
        return (grad_in, sketch)

    first_mixed = mix(rows_in, 0, own_dilation)
    section_out = (
        rows_in.astype(jnp.float32)
        + jnp.dot(first_mixed, full_weights[0], preferred_element_type=jnp.float32)
    ).astype(jnp.bfloat16)
    half = width // 2
    received = passed_along(section_out, "segment", 1)
    late_mixed = mix(received, late_index, own_dilation)
    grad_late, sketch_late = backward(received, late_mixed, grad_out, late_index, own_dilation)
    grad_back = passed_along(grad_late, "segment", -1)
    grad_early, sketch_early = backward(rows_in, first_mixed, grad_back, 0, own_dilation)
    local_sketch = jnp.where(segment_index == 1, sketch_late, sketch_early)
    moved = passed_along(grad_early[:, half:], "segment", 1)
    grad_half = jnp.where(segment_index == 0, grad_early[:, :half], moved)
    summed = lax.psum_scatter(
        local_sketch.astype(jnp.bfloat16), "ctx", scatter_dimension=0, tiled=True
    )
    merged = lax.psum(summed, "dp").astype(jnp.float32)
    return (grad_half[None], merged[None])


def solution(mesh):
    in_specs = (
        P("dp", "ctx", None),
        P("dp", "ctx", None),
        P("segment", "ctx", None),
        P("segment", None, None),
        P("segment", None, None),
        P(),
    )
    out_specs = (P("dp", "ctx", "segment"), P("segment", "ctx", None))
    return jax.shard_map(shards, mesh=mesh, in_specs=in_specs, out_specs=out_specs, check_vma=False)
```

profile of v0, /device:TPU:0, one launch (start us, length us, event | category | flops | bytes accessed | tf_op | source)
XLA Modules:
  0.0 245.8 jit_solution(9777423108458225322)
XLA Ops:
  7.2 0.0 copy-start
  7.2 0.0 all-gather.2.cloned.1.call-start
  7.2 0.7 all-gather.2.cloned.1.call-update
  7.9 0.0 copy-start.12
  7.9 0.0 copy-start.9
  7.9 0.0 reduce-scatter.2.cloned.1.call-start
  8.0 1.4 fusion.52
  9.4 0.6 copy-done.10
  9.9 0.0 copy-done.1
  9.9 0.7 fusion.49
  10.6 4.9 %collective-permute-start.2 = (bf16[64,1536]{1,0:T(8,128)(2,1)S(1)}, bf16[64,1536]{1,0:T(8,128)(2,1)S(1)}, u32[]{:S(2)}, u32[]{:S(2)}) collective-permute-start(bf16[64,1536]{1,0:T(8,128)(2,1)S(1)} %get-tuple-element.16), channel_id=1, source_target_pairs={{0,2},{2,4},{4,6},{6,8},{8,10},{10,12},{12,14},{1,3},{3,5},{5,7},{... | collective-permute-start | bytes 589832 | tf_op jit(solution)/shard_map/ppermute | solution.py:16
  15.5 1.3 collective-permute-start.3
  16.9 0.6 fusion.77
  18.8 0.1 slice_reduce_fusion.2
  18.8 0.9 collective-permute-done.2
  19.8 4.1 %collective-permute-done.3 = bf16[64,1536]{1,0:T(8,128)(2,1)S(1)} collective-permute-done((bf16[64,1536]{1,0:T(8,128)(2,1)S(1)}, bf16[64,1536]{1,0:T(8,128)(2,1)S(1)}, u32[]{:S(2)}, u32[]{:S(2)}) %collective-permute-start.3) | collective-permute-done | bytes 196640 | tf_op jit(solution)/shard_map/ppermute | solution.py:17
  23.9 0.1 pad_maximum_fusion.1
  24.0 0.0 copy-done.7
  24.0 1.2 add_convert_fusion.1
  25.2 0.0 copy-start.3
  25.2 67.2 %all-gather.2.cloned.1.call-done = bf16[1,1536,1536]{2,1,0:T(8,128)(2,1)} async-done(((bf16[1,192,1536]{2,1,0:T(8,128)(2,1)}), bf16[1,1536,1536]{2,1,0:T(8,128)(2,1)}) %all-gather.2.cloned.1.call-update) | async-done | bytes 4718608 | tf_op jit(solution)/shard_map/all_gather | solution.py:49
  92.4 3.9 %fusion.19 = bf16[256,1536]{1,0:T(8,128)(2,1)S(1)} fusion(bf16[256,1536]{1,0:T(8,128)(2,1)S(1)} %add_convert_fusion.1, bf16[1,1536,1536]{2,1,0:T(8,128)(2,1)} %all-gather.2.cloned.1.call-done, bf16[1,256,1536]{2,1,0:T(8,128)(2,1)S(1)} %copy-done.1), kind=kOutput, calls=%fused_computation.27 | convolution fusion | flops 1209139200 | bytes 7077888 | tf_op jit(solution)/shard_map/dot_general | solution.py:90
  96.2 1.3 collective-permute-start.4
  97.6 0.0 copy-done.3
  97.6 0.0 copy-done.13
  97.6 1.4 fusion.22
  99.1 2.5 %collective-permute-start = (bf16[64,1536]{1,0:T(8,128)(2,1)S(1)}, bf16[64,1536]{1,0:T(8,128)(2,1)S(1)}, u32[]{:S(2)}, u32[]{:S(2)}) collective-permute-start(bf16[64,1536]{1,0:T(8,128)(2,1)S(1)} %get-tuple-element.14), channel_id=1, source_target_pairs={{0,2},{2,4},{4,6},{6,8},{8,10},{10,12},{12,14},{1,3},{3,5},{5,7},{... | collective-permute-start | bytes 589832 | tf_op jit(solution)/shard_map/ppermute | solution.py:16
  101.5 1.3 collective-permute-start.1
  102.8 4.0 %collective-permute-done = bf16[64,1536]{1,0:T(8,128)(2,1)S(1)} collective-permute-done((bf16[64,1536]{1,0:T(8,128)(2,1)S(1)}, bf16[64,1536]{1,0:T(8,128)(2,1)S(1)}, u32[]{:S(2)}, u32[]{:S(2)}) %collective-permute-start) | collective-permute-done | bytes 196640 | tf_op jit(solution)/shard_map/ppermute | solution.py:16
  106.8 2.3 collective-permute-done.1
  109.1 0.1 pad_maximum_fusion
  109.2 0.0 collective-permute-done.4
  109.2 0.2 fusion.44
  109.5 0.0 copy-start.4
  109.5 2.5 %fusion.45 = (f32[256]{0:T(256)S(1)}, f32[256,1536]{1,0:T(8,128)S(1)}, bf16[256,1536]{1,0:T(8,128)(2,1)S(1)}) fusion(bf16[256,1536]{1,0:T(8,128)(2,1)S(1)} %collective-permute-done.4, f32[256]{0:T(256)S(1)} %fusion.70, bf16[384,1536]{1,0:T(8,128)(2,1)S(1)} %pad_maximum_fusion, s32[]{:T(128)S(6)} %select_n.35, f32[1536]{0:T(1024)S(1)} %get-tuple-element.3, ...), kind=kLoop, calls=%fused_computation.49 | loop fusion | flops 12975872 | bytes 5525512 | tf_op jit(solution)/shard_map/transpose(jvp())/reduce_sum | solution.py:29
  112.0 1.4 fusion.35
  113.3 1.3 collective-permute-start.5
  114.6 0.8 fusion.73
  115.4 4.6 %collective-permute-start.9 = (bf16[64,1536]{1,0:T(8,128)(2,1)}, bf16[64,1536]{1,0:T(8,128)(2,1)S(1)}, u32[]{:S(2)}, u32[]{:S(2)}) collective-permute-start(bf16[64,1536]{1,0:T(8,128)(2,1)} %get-tuple-element.10), channel_id=1, source_target_pairs={{0,2},{2,4},{4,6},{6,8},{8,10},{10,12},{12,14},{1,3},{3,5},{5,7},{... | collective-permute-start | bytes 589832 | tf_op jit(solution)/shard_map/ppermute | solution.py:16
  120.0 1.3 collective-permute-start.10
  121.3 4.1 %collective-permute-done.9 = bf16[64,1536]{1,0:T(8,128)(2,1)S(1)} collective-permute-done((bf16[64,1536]{1,0:T(8,128)(2,1)}, bf16[64,1536]{1,0:T(8,128)(2,1)S(1)}, u32[]{:S(2)}, u32[]{:S(2)}) %collective-permute-start.9) | collective-permute-done | bytes 196640 | tf_op jit(solution)/shard_map/ppermute | solution.py:16
  125.4 4.4 %collective-permute-done.10 = bf16[64,1536]{1,0:T(8,128)(2,1)S(1)} collective-permute-done((bf16[64,1536]{1,0:T(8,128)(2,1)}, bf16[64,1536]{1,0:T(8,128)(2,1)S(1)}, u32[]{:S(2)}, u32[]{:S(2)}) %collective-permute-start.10) | collective-permute-done | bytes 196640 | tf_op jit(solution)/shard_map/ppermute | solution.py:17
  129.8 1.1 pad_maximum_fusion.3
  130.9 3.9 %fusion.54 = bf16[256,1536]{1,0:T(8,128)(2,1)} fusion(bf16[256,1536]{1,0:T(8,128)(2,1)S(1)} %get-tuple-element.9, bf16[1,1536,256]{2,1,0:T(8,128)(2,1)S(1)} %copy-done, bf16[1,256,1536]{2,1,0:T(8,128)(2,1)} %param.7, bf16[384,1536]{1,0:T(8,128)(2,1)} %pad_maximum_fusion.3, s32[]{:T(128)S(6)} %select_n.34, s32[]{:T(128)S(6)} %select_n.35, ...), kind=kOutput, calls=%fused_computation.66 | convolution fusion | flops 406257664 | bytes 4739080 | tf_op jit(solution)/shard_map/dot_general | solution.py:82
  134.8 0.0 collective-permute-done.5
  134.8 3.7 %fusion.25 = bf16[256,1536]{1,0:T(8,128)(2,1)S(1)} fusion(bf16[256,1536]{1,0:T(8,128)(2,1)S(1)} %collective-permute-done.5, bf16[1,1536,1536]{2,1,0:T(8,128)(2,1)} %all-gather.2.cloned.1.call-done), kind=kOutput, calls=%fused_computation.29 | convolution fusion | flops 1208352768 | bytes 6291456 | tf_op jit(solution)/shard_map/dot_general | solution.py:52
  138.6 0.8 fusion.74
  139.4 4.7 %collective-permute-start.6 = (bf16[64,1536]{1,0:T(8,128)(2,1)}, bf16[64,1536]{1,0:T(8,128)(2,1)S(1)}, u32[]{:S(2)}, u32[]{:S(2)}) collective-permute-start(bf16[64,1536]{1,0:T(8,128)(2,1)} %get-tuple-element.12), channel_id=1, source_target_pairs={{0,2},{2,4},{4,6},{6,8},{8,10},{10,12},{12,14},{1,3},{3,5},{5,7},{... | collective-permute-start | bytes 589832 | tf_op jit(solution)/shard_map/ppermute | solution.py:16
  144.1 1.3 collective-permute-start.7
  145.4 3.2 %fusion.18 = bf16[256,1536]{1,0:T(8,128)(2,1)} fusion(bf16[256,1536]{1,0:T(8,128)(2,1)} %fusion.54, bf16[256,1536]{1,0:T(8,128)(2,1)} %copy-done.2, bf16[256,1536]{1,0:T(8,128)(2,1)S(1)} %collective-permute-done.5, bf16[1,1536,256]{2,1,0:T(8,128)(2,1)S(1)} %copy-done, pred[]{:T(512)S(6)} %eq.8), kind=kOutput, calls=%fused_computation.26 | convolution fusion | flops 403111936 | bytes 3932161 | tf_op jit(solution)/shard_map/dot_general | solution.py:82
  148.6 0.0 reduce-scatter.2.cloned.1.call-update
  148.6 0.2 all-reduce.2.cloned.1.call-start
  148.8 0.0 collective-permute-done.6
  148.8 4.6 %collective-permute-done.7 = bf16[64,1536]{1,0:T(8,128)(2,1)S(1)} collective-permute-done((bf16[64,1536]{1,0:T(8,128)(2,1)}, bf16[64,1536]{1,0:T(8,128)(2,1)S(1)}, u32[]{:S(2)}, u32[]{:S(2)}) %collective-permute-start.7) | collective-permute-done | bytes 196640 | tf_op jit(solution)/shard_map/ppermute | solution.py:17
  153.4 0.1 pad_maximum_fusion.2
  153.6 2.4 fusion.53
  155.9 0.5 fusion.37
  156.4 1.3 collective-permute-start.8
  157.8 57.4 %reduce-scatter.2.cloned.1.call-done = bf16[32,1536]{1,0:T(8,128)(2,1)} async-done(((bf16[256,1536]{1,0:T(8,128)(2,1)}), bf16[32,1536]{1,0:T(8,128)(2,1)}) %reduce-scatter.2.cloned.1.call-update) | async-done | bytes 98320 | tf_op jit(solution)/shard_map/reduce_scatter | solution.py:101
  215.2 0.0 all-reduce.2.cloned.1.call-update
  215.2 0.0 collective-permute-done.8
  215.2 0.8 fusion.67
  216.0 21.7 %all-reduce.2.cloned.1.call-done = bf16[1,32,1536]{2,1,0:T(8,128)(2,1)} async-done(((bf16[1,32,1536]{2,1,0:T(8,128)(2,1)}), bf16[1,32,1536]{2,1,0:T(8,128)(2,1)}) %all-reduce.2.cloned.1.call-update) | async-done | bytes 98320 | tf_op jit(solution)/shard_map/psum | solution.py:104
  237.7 1.6 broadcast_in_dim.23
  (25 shorter events, 0.2 us)
Async XLA Ops:
  7.2 123.8 %copy-start = (bf16[1,1536,256]{2,1,0:T(8,128)(2,1)S(1)}, bf16[1,1536,256]{2,1,0:T(8,128)(2,1)}, u32[]{:S(2)}) copy-start(bf16[1,1536,256]{2,1,0:T(8,128)(2,1)} %param.10) | copy-start | bytes 2359300
  7.2 2.8 %copy-start.1 = (bf16[1,256,1536]{2,1,0:T(8,128)(2,1)S(1)}, bf16[1,256,1536]{2,1,0:T(8,128)(2,1)}, u32[]{:S(2)}) copy-start(bf16[1,256,1536]{2,1,0:T(8,128)(2,1)} %param.6) | copy-start | bytes 2359300
  7.2 85.2 %all-gather.2.cloned.1.call-start = ((), (), s32[]{:S(2)}) async-start(), calls=%async_computation.1 | async-start | bytes 5308416 | tf_op jit(solution)/shard_map/all_gather | solution.py:49
  7.9 8.9 %copy-start.12 = (s32[2]{0:T(128)S(1)}, s32[2]{0:T(128)}, u32[]{:S(2)}) copy-start(s32[2]{0:T(128)} %param.11) | copy-start | bytes 28
  7.9 10.8 %copy-start.9 = (f32[1,3,1536]{2,0,1:T(1,128)S(1)}, f32[1,3,1536]{2,0,1:T(1,128)}, u32[]{:S(2)}) copy-start(f32[1,3,1536]{2,0,1:T(1,128)} %param.9) | copy-start | bytes 55300
  7.9 207.2 %reduce-scatter.2.cloned.1.call-start = ((), (), s32[]{:S(2)}) async-start(), calls=%async_computation.2 | async-start | bytes 884736 | tf_op jit(solution)/shard_map/reduce_scatter | solution.py:101
  9.4 0.6 copy-start.10
  9.9 14.0 %copy-start.7 = (f32[256]{0:T(256)}, f32[256]{0:T(256)S(1)}, u32[]{:S(2)}) copy-start(f32[256]{0:T(256)S(1)} %fusion.69) | copy-start | bytes 3076
  10.6 9.1 %collective-permute-start.2 = (bf16[64,1536]{1,0:T(8,128)(2,1)S(1)}, bf16[64,1536]{1,0:T(8,128)(2,1)S(1)}, u32[]{:S(2)}, u32[]{:S(2)}) collective-permute-start(bf16[64,1536]{1,0:T(8,128)(2,1)S(1)} %get-tuple-element.16), channel_id=1, source_target_pairs={{0,2},{2,4},{4,6},{6,8},{8,10},{10,12},{12,14},{1,3},{3,5},{5,7},{... | collective-permute-start | bytes 589832 | tf_op jit(solution)/shard_map/ppermute | solution.py:16
  15.5 8.3 %collective-permute-start.3 = (bf16[64,1536]{1,0:T(8,128)(2,1)S(1)}, bf16[64,1536]{1,0:T(8,128)(2,1)S(1)}, u32[]{:S(2)}, u32[]{:S(2)}) collective-permute-start(bf16[64,1536]{1,0:T(8,128)(2,1)S(1)} %get-tuple-element.17), channel_id=1, source_target_pairs={{2,0},{4,2},{6,4},{8,6},{10,8},{12,10},{14,12},{3,1},{5,3},{7,5},{... | collective-permute-start | bytes 589832 | tf_op jit(solution)/shard_map/ppermute | solution.py:17
  18.8 90.6 %copy-start.5 = (f32[1536]{0:T(1024)}, f32[1536]{0:T(1024)S(1)}, u32[]{:S(2)}) copy-start(f32[1536]{0:T(1024)S(1)} %get-tuple-element.4) | copy-start | bytes 18436
  25.2 71.1 %copy-start.2 = (bf16[256,1536]{1,0:T(8,128)(2,1)}, bf16[256,1536]{1,0:T(8,128)(2,1)S(1)}, u32[]{:S(2)}) copy-start(bf16[256,1536]{1,0:T(8,128)(2,1)S(1)} %add_convert_fusion.1) | copy-start | bytes 2359300
  25.2 72.4 %copy-start.3 = (bf16[1,256,1536]{2,1,0:T(8,128)(2,1)S(1)}, bf16[1,256,1536]{2,1,0:T(8,128)(2,1)}, u32[]{:S(2)}) copy-start(bf16[1,256,1536]{2,1,0:T(8,128)(2,1)} %param.7) | copy-start | bytes 2359300
  92.4 5.2 %copy-start.13 = (bf16[1,1536,1536]{2,1,0:T(8,128)(2,1)S(1)}, bf16[1,1536,1536]{2,1,0:T(8,128)(2,1)}, u32[]{:S(2)}) copy-start(bf16[1,1536,1536]{2,1,0:T(8,128)(2,1)} %all-gather.2.cloned.1.call-done) | copy-start | bytes 14155780
  96.2 13.0 %collective-permute-start.4 = (bf16[256,1536]{1,0:T(8,128)(2,1)S(1)}, bf16[256,1536]{1,0:T(8,128)(2,1)S(1)}, u32[]{:S(2)}, u32[]{:S(2)}) collective-permute-start(bf16[256,1536]{1,0:T(8,128)(2,1)S(1)} %fusion.19), channel_id=1, source_target_pairs={{0,1},{2,3},{4,5},{6,7},{8,9},{10,11},{12,13},{14,15},{16,17},{18,... | collective-permute-start | bytes 2359304 | tf_op jit(solution)/shard_map/ppermute | solution.py:25
  99.1 7.8 %collective-permute-start = (bf16[64,1536]{1,0:T(8,128)(2,1)S(1)}, bf16[64,1536]{1,0:T(8,128)(2,1)S(1)}, u32[]{:S(2)}, u32[]{:S(2)}) collective-permute-start(bf16[64,1536]{1,0:T(8,128)(2,1)S(1)} %get-tuple-element.14), channel_id=1, source_target_pairs={{0,2},{2,4},{4,6},{6,8},{8,10},{10,12},{12,14},{1,3},{3,5},{5,7},{... | collective-permute-start | bytes 589832 | tf_op jit(solution)/shard_map/ppermute | solution.py:16
  101.5 7.6 %collective-permute-start.1 = (bf16[64,1536]{1,0:T(8,128)(2,1)S(1)}, bf16[64,1536]{1,0:T(8,128)(2,1)S(1)}, u32[]{:S(2)}, u32[]{:S(2)}) collective-permute-start(bf16[64,1536]{1,0:T(8,128)(2,1)S(1)} %get-tuple-element.15), channel_id=1, source_target_pairs={{2,0},{4,2},{6,4},{8,6},{10,8},{12,10},{14,12},{3,1},{5,3},{7,5},{... | collective-permute-start | bytes 589832 | tf_op jit(solution)/shard_map/ppermute | solution.py:17
  109.5 2.5 %copy-start.4 = (bf16[1,256,1536]{2,1,0:T(8,128)(2,1)S(1)}, bf16[1,256,1536]{2,1,0:T(8,128)(2,1)}, u32[]{:S(2)}) copy-start(bf16[1,256,1536]{2,1,0:T(8,128)(2,1)} %param.7) | copy-start | bytes 2359300
  113.3 21.5 %collective-permute-start.5 = (bf16[256,1536]{1,0:T(8,128)(2,1)}, bf16[256,1536]{1,0:T(8,128)(2,1)S(1)}, u32[]{:S(2)}, u32[]{:S(2)}) collective-permute-start(bf16[256,1536]{1,0:T(8,128)(2,1)} %fusion.35), channel_id=1, source_target_pairs={{1,0},{3,2},{5,4},{7,6},{9,8},{11,10},{13,12},{15,14},{17,16},{19,... | collective-permute-start | bytes 2359304 | tf_op jit(solution)/shard_map/ppermute | solution.py:25
  115.4 10.0 %collective-permute-start.9 = (bf16[64,1536]{1,0:T(8,128)(2,1)}, bf16[64,1536]{1,0:T(8,128)(2,1)S(1)}, u32[]{:S(2)}, u32[]{:S(2)}) collective-permute-start(bf16[64,1536]{1,0:T(8,128)(2,1)} %get-tuple-element.10), channel_id=1, source_target_pairs={{0,2},{2,4},{4,6},{6,8},{8,10},{10,12},{12,14},{1,3},{3,5},{5,7},{... | collective-permute-start | bytes 589832 | tf_op jit(solution)/shard_map/ppermute | solution.py:16
  120.0 9.8 %collective-permute-start.10 = (bf16[64,1536]{1,0:T(8,128)(2,1)}, bf16[64,1536]{1,0:T(8,128)(2,1)S(1)}, u32[]{:S(2)}, u32[]{:S(2)}) collective-permute-start(bf16[64,1536]{1,0:T(8,128)(2,1)} %get-tuple-element.11), channel_id=1, source_target_pairs={{2,0},{4,2},{6,4},{8,6},{10,8},{12,10},{14,12},{3,1},{5,3},{7,5},{... | collective-permute-start | bytes 589832 | tf_op jit(solution)/shard_map/ppermute | solution.py:17
  139.4 9.5 %collective-permute-start.6 = (bf16[64,1536]{1,0:T(8,128)(2,1)}, bf16[64,1536]{1,0:T(8,128)(2,1)S(1)}, u32[]{:S(2)}, u32[]{:S(2)}) collective-permute-start(bf16[64,1536]{1,0:T(8,128)(2,1)} %get-tuple-element.12), channel_id=1, source_target_pairs={{0,2},{2,4},{4,6},{6,8},{8,10},{10,12},{12,14},{1,3},{3,5},{5,7},{... | collective-permute-start | bytes 589832 | tf_op jit(solution)/shard_map/ppermute | solution.py:16
  144.1 9.4 %collective-permute-start.7 = (bf16[64,1536]{1,0:T(8,128)(2,1)}, bf16[64,1536]{1,0:T(8,128)(2,1)S(1)}, u32[]{:S(2)}, u32[]{:S(2)}) collective-permute-start(bf16[64,1536]{1,0:T(8,128)(2,1)} %get-tuple-element.13), channel_id=1, source_target_pairs={{2,0},{4,2},{6,4},{8,6},{10,8},{12,10},{14,12},{3,1},{5,3},{7,5},{... | collective-permute-start | bytes 589832 | tf_op jit(solution)/shard_map/ppermute | solution.py:17
  148.6 89.1 %all-reduce.2.cloned.1.call-start = ((), (), s32[]{:S(2)}) async-start(), calls=%async_computation.3 | async-start | bytes 196608 | tf_op jit(solution)/shard_map/psum | solution.py:104
  148.8 4.7 %copy-start.6 = (f32[1536]{0:T(1024)S(1)}, f32[1536]{0:T(1024)}, u32[]{:S(2)}) copy-start(f32[1536]{0:T(1024)} %copy-done.5) | copy-start | bytes 18436
  148.8 4.7 %copy-start.8 = (f32[256]{0:T(256)S(1)}, f32[256]{0:T(256)}, u32[]{:S(2)}) copy-start(f32[256]{0:T(256)} %copy-done.7) | copy-start | bytes 3076
  153.5 2.4 copy-start.11
  156.4 58.8 %collective-permute-start.8 = (bf16[256,768]{1,0:T(8,128)(2,1)S(1)}, bf16[256,768]{1,0:T(8,128)(2,1)S(1)}, u32[]{:S(2)}, u32[]{:S(2)}) collective-permute-start(bf16[256,768]{1,0:T(8,128)(2,1)S(1)} %slice.79), channel_id=1, source_target_pairs={{0,1},{2,3},{4,5},{6,7},{8,9},{10,11},{12,13},{14,15},{16,17},{18,... | collective-permute-start | bytes 1179656 | tf_op jit(solution)/shard_map/ppermute | solution.py:25
Sparse Core Ops, SparseCore 0:
  10.2 82.1 all-gather.1
  148.7 66.4 reduce-scatter.1
  217.4 20.2 all-reduce.1
where the time goes:
time: 246 us
  waiting for transfers between devices  171 us (70%)
  starting transfers between devices  26.1 us (11%)
  matrix products  16.1 us (7%)
  between operations  15.4 us (6%)
  other arithmetic  13.9 us (6%)
  local copies, waits for them, and re-layouts  2.89 us (1%)
    all_gather x1, waiting for transfers between devices, shards(): full_weights = lax.all_gather(pair_weights, 'ctx', axis=1, tiled=True)  67.2 us
    reduce_scatter x1, waiting for transfers between devices, shards(): lax.psum_scatter(local_sketch.astype(jnp.bfloat16), 'ctx', scatter_dimens...  57.4 us
    psum x1, waiting for transfers between devices, shards(): merged = lax.psum(summed, 'dp').astype(jnp.float32)  21.7 us
    ppermute x4, starting transfers between devices, with_halo(): before = lax.ppermute(last, axis, up)  16.7 us
    ppermute x4, waiting for transfers between devices, with_halo(): after = lax.ppermute(leading, axis, down)  15.4 us
    ppermute x4, waiting for transfers between devices, with_halo(): before = lax.ppermute(last, axis, up)  8.97 us
    dot_general x2, matrix products, backward(): lax.dot_general(sketched, mixed, (((0,), (0,)), ((), ())), preferred_elem...  7.08 us
    ppermute x4, starting transfers between devices, with_halo(): after = lax.ppermute(leading, axis, down)  5.17 us
  transfers between devices with their start and end apart: 14, of which 10 were waited for; matrix products, arithmetic and copies ran while one was open for 7% of the time, Pallas kernels for 0%

commit v1 on v0

--- a/solution.py
+++ b/solution.py
@@ -101,7 +101,11 @@
     summed = lax.psum_scatter(
         local_sketch.astype(jnp.bfloat16), "ctx", scatter_dimension=0, tiled=True
     )
-    merged = lax.psum(summed, "dp").astype(jnp.float32)
+
+    def mix_the_edge(x0):
+        return jnp.sum(lax.all_gather(x0, "dp"), axis=0)
+
+    merged = mix_the_edge(summed).astype(jnp.float32)
     return (grad_half[None], merged[None])
 
 

time: 246 us -> 229 us (0.931)
  waiting for transfers between devices: 171 us -> 149 us
  blocking collectives: 0 us -> 5.48 us
    psum x1 -> x0, waiting for transfers between devices: 21.7 us -> none  [shards(): merged = lax.psum(summed, 'dp').astype(jnp.float32)]
    all_gather x0 -> x1, blocking collectives: none -> 5.48 us  [mix_the_edge(): return jnp.sum(lax.all_gather(x0, 'dp'), axis=0)]
  transfers between devices with their start and end apart: 14 -> 13, of which waited for: 10 -> 10; matrix products, arithmetic and copies ran while one was open for 7% -> 8% of each run, Pallas kernels for 0% -> 0%
where the time goes in v1:
time: 229 us; the launch traced here: 228 us
  waiting for transfers between devices  149 us (65%)
  starting transfers between devices  26 us (11%)
  matrix products  16.1 us (7%)
  between operations  15.7 us (7%)
  other arithmetic  13.1 us (6%)
  blocking collectives  5.48 us (2%)
  local copies, waits for them, and re-layouts  2.88 us (1%)
    all_gather x1, waiting for transfers between devices, shards(): full_weights = lax.all_gather(pair_weights, 'ctx', axis=1, tiled=True)  67.2 us
    reduce_scatter x1, waiting for transfers between devices, shards(): lax.psum_scatter(local_sketch.astype(jnp.bfloat16), 'ctx', scatter_dimens...  55.5 us
    ppermute x4, starting transfers between devices, with_halo(): before = lax.ppermute(last, axis, up)  16.7 us
    ppermute x4, waiting for transfers between devices, with_halo(): after = lax.ppermute(leading, axis, down)  15.5 us
    ppermute x4, waiting for transfers between devices, with_halo(): before = lax.ppermute(last, axis, up)  8.97 us
    dot_general x2, matrix products, backward(): lax.dot_general(sketched, mixed, (((0,), (0,)), ((), ())), preferred_elem...  7.07 us
    all_gather x1, blocking collectives, mix_the_edge(): return jnp.sum(lax.all_gather(x0, 'dp'), axis=0)  5.48 us
    ppermute x4, starting transfers between devices, with_halo(): after = lax.ppermute(leading, axis, down)  5.35 us
  transfers between devices with their start and end apart: 13, of which 10 were waited for; matrix products, arithmetic and copies ran while one was open for 8% of the time, Pallas kernels for 0%

profile of v1, /device:TPU:0, one launch (start us, length us, event | category | flops | bytes accessed | tf_op | source)
XLA Modules:
  0.0 228.4 jit_solution(9061317051728726887)
XLA Ops:
  7.2 0.0 copy-start
  7.2 0.0 all-gather.3.cloned.1.call-start
  7.2 0.7 all-gather.3.cloned.1.call-update
  7.9 0.0 copy-start.12
  7.9 0.0 copy-start.9
  7.9 0.0 reduce-scatter.2.cloned.1.call-start
  8.0 1.4 fusion.52
  9.4 0.6 copy-done.10
  9.9 0.0 copy-done.1
  9.9 0.7 fusion.49
  10.6 4.9 %collective-permute-start.2 = (bf16[64,1536]{1,0:T(8,128)(2,1)S(1)}, bf16[64,1536]{1,0:T(8,128)(2,1)S(1)}, u32[]{:S(2)}, u32[]{:S(2)}) collective-permute-start(bf16[64,1536]{1,0:T(8,128)(2,1)S(1)} %get-tuple-element.16), channel_id=1, source_target_pairs={{0,2},{2,4},{4,6},{6,8},{8,10},{10,12},{12,14},{1,3},{3,5},{5,7},{... | collective-permute-start | bytes 589832 | tf_op jit(solution)/shard_map/ppermute | solution.py:16
  15.5 1.3 collective-permute-start.3
  16.8 0.6 fusion.77
  18.7 0.1 slice_reduce_fusion.2
  18.8 0.0 copy-start.5
  18.8 0.9 collective-permute-done.2
  19.7 4.1 %collective-permute-done.3 = bf16[64,1536]{1,0:T(8,128)(2,1)S(1)} collective-permute-done((bf16[64,1536]{1,0:T(8,128)(2,1)S(1)}, bf16[64,1536]{1,0:T(8,128)(2,1)S(1)}, u32[]{:S(2)}, u32[]{:S(2)}) %collective-permute-start.3) | collective-permute-done | bytes 196640 | tf_op jit(solution)/shard_map/ppermute | solution.py:17
  23.9 0.1 pad_maximum_fusion.1
  23.9 1.2 add_convert_fusion.1
  25.1 0.0 copy-start.2
  25.2 0.0 copy-start.3
  25.2 67.2 %all-gather.3.cloned.1.call-done = bf16[1,1536,1536]{2,1,0:T(8,128)(2,1)} async-done(((bf16[1,192,1536]{2,1,0:T(8,128)(2,1)}), bf16[1,1536,1536]{2,1,0:T(8,128)(2,1)}) %all-gather.3.cloned.1.call-update) | async-done | bytes 4718608 | tf_op jit(solution)/shard_map/all_gather | solution.py:49
  92.4 3.9 %fusion.19 = bf16[256,1536]{1,0:T(8,128)(2,1)S(1)} fusion(bf16[256,1536]{1,0:T(8,128)(2,1)S(1)} %add_convert_fusion.1, bf16[1,1536,1536]{2,1,0:T(8,128)(2,1)} %all-gather.3.cloned.1.call-done, bf16[1,256,1536]{2,1,0:T(8,128)(2,1)S(1)} %copy-done.1), kind=kOutput, calls=%fused_computation.27 | convolution fusion | flops 1209139200 | bytes 7077888 | tf_op jit(solution)/shard_map/dot_general | solution.py:90
  96.2 1.3 collective-permute-start.4
  97.6 1.4 fusion.22
  99.1 2.5 %collective-permute-start = (bf16[64,1536]{1,0:T(8,128)(2,1)S(1)}, bf16[64,1536]{1,0:T(8,128)(2,1)S(1)}, u32[]{:S(2)}, u32[]{:S(2)}) collective-permute-start(bf16[64,1536]{1,0:T(8,128)(2,1)S(1)} %get-tuple-element.14), channel_id=1, source_target_pairs={{0,2},{2,4},{4,6},{6,8},{8,10},{10,12},{12,14},{1,3},{3,5},{5,7},{... | collective-permute-start | bytes 589832 | tf_op jit(solution)/shard_map/ppermute | solution.py:16
  101.5 1.3 collective-permute-start.1
  102.8 4.0 %collective-permute-done = bf16[64,1536]{1,0:T(8,128)(2,1)S(1)} collective-permute-done((bf16[64,1536]{1,0:T(8,128)(2,1)S(1)}, bf16[64,1536]{1,0:T(8,128)(2,1)S(1)}, u32[]{:S(2)}, u32[]{:S(2)}) %collective-permute-start) | collective-permute-done | bytes 196640 | tf_op jit(solution)/shard_map/ppermute | solution.py:16
  106.8 2.3 %collective-permute-done.1 = bf16[64,1536]{1,0:T(8,128)(2,1)S(1)} collective-permute-done((bf16[64,1536]{1,0:T(8,128)(2,1)S(1)}, bf16[64,1536]{1,0:T(8,128)(2,1)S(1)}, u32[]{:S(2)}, u32[]{:S(2)}) %collective-permute-start.1) | collective-permute-done | bytes 196640 | tf_op jit(solution)/shard_map/ppermute | solution.py:17
  109.1 0.1 pad_maximum_fusion
  109.2 0.0 collective-permute-done.4
  109.2 0.2 fusion.44
  109.4 0.0 copy-start.4
  109.5 2.5 %fusion.45 = (f32[256]{0:T(256)S(1)}, f32[256,1536]{1,0:T(8,128)S(1)}, bf16[256,1536]{1,0:T(8,128)(2,1)S(1)}) fusion(bf16[256,1536]{1,0:T(8,128)(2,1)S(1)} %collective-permute-done.4, f32[256]{0:T(256)S(1)} %fusion.70, bf16[384,1536]{1,0:T(8,128)(2,1)S(1)} %pad_maximum_fusion, s32[]{:T(128)S(6)} %select_n.35, f32[1536]{0:T(1024)S(1)} %get-tuple-element.3, ...), kind=kLoop, calls=%fused_computation.49 | loop fusion | flops 12975872 | bytes 5525512 | tf_op jit(solution)/shard_map/transpose(jvp())/reduce_sum | solution.py:29
  112.0 0.0 copy-done.4
  112.0 1.4 fusion.35
  113.3 1.3 collective-permute-start.5
  114.6 0.8 fusion.73
  115.4 4.6 %collective-permute-start.9 = (bf16[64,1536]{1,0:T(8,128)(2,1)}, bf16[64,1536]{1,0:T(8,128)(2,1)S(1)}, u32[]{:S(2)}, u32[]{:S(2)}) collective-permute-start(bf16[64,1536]{1,0:T(8,128)(2,1)} %get-tuple-element.10), channel_id=1, source_target_pairs={{0,2},{2,4},{4,6},{6,8},{8,10},{10,12},{12,14},{1,3},{3,5},{5,7},{... | collective-permute-start | bytes 589832 | tf_op jit(solution)/shard_map/ppermute | solution.py:16
  120.0 1.3 collective-permute-start.10
  121.3 4.1 %collective-permute-done.9 = bf16[64,1536]{1,0:T(8,128)(2,1)S(1)} collective-permute-done((bf16[64,1536]{1,0:T(8,128)(2,1)}, bf16[64,1536]{1,0:T(8,128)(2,1)S(1)}, u32[]{:S(2)}, u32[]{:S(2)}) %collective-permute-start.9) | collective-permute-done | bytes 196640 | tf_op jit(solution)/shard_map/ppermute | solution.py:16
  125.4 4.4 %collective-permute-done.10 = bf16[64,1536]{1,0:T(8,128)(2,1)S(1)} collective-permute-done((bf16[64,1536]{1,0:T(8,128)(2,1)}, bf16[64,1536]{1,0:T(8,128)(2,1)S(1)}, u32[]{:S(2)}, u32[]{:S(2)}) %collective-permute-start.10) | collective-permute-done | bytes 196640 | tf_op jit(solution)/shard_map/ppermute | solution.py:17
  129.8 1.1 pad_maximum_fusion.3
  131.0 0.0 copy-done
  131.0 3.9 %fusion.54 = bf16[256,1536]{1,0:T(8,128)(2,1)} fusion(bf16[256,1536]{1,0:T(8,128)(2,1)S(1)} %get-tuple-element.9, bf16[1,1536,256]{2,1,0:T(8,128)(2,1)S(1)} %copy-done, bf16[1,256,1536]{2,1,0:T(8,128)(2,1)} %param.7, bf16[384,1536]{1,0:T(8,128)(2,1)} %pad_maximum_fusion.3, s32[]{:T(128)S(6)} %select_n.34, s32[]{:T(128)S(6)} %select_n.35, ...), kind=kOutput, calls=%fused_computation.66 | convolution fusion | flops 406257664 | bytes 4739080 | tf_op jit(solution)/shard_map/dot_general | solution.py:82
  134.9 0.0 collective-permute-done.5
  134.9 3.7 %fusion.25 = bf16[256,1536]{1,0:T(8,128)(2,1)S(1)} fusion(bf16[256,1536]{1,0:T(8,128)(2,1)S(1)} %collective-permute-done.5, bf16[1,1536,1536]{2,1,0:T(8,128)(2,1)} %all-gather.3.cloned.1.call-done), kind=kOutput, calls=%fused_computation.29 | convolution fusion | flops 1208352768 | bytes 6291456 | tf_op jit(solution)/shard_map/dot_general | solution.py:52
  138.6 0.8 fusion.74
  139.4 4.7 %collective-permute-start.6 = (bf16[64,1536]{1,0:T(8,128)(2,1)}, bf16[64,1536]{1,0:T(8,128)(2,1)S(1)}, u32[]{:S(2)}, u32[]{:S(2)}) collective-permute-start(bf16[64,1536]{1,0:T(8,128)(2,1)} %get-tuple-element.12), channel_id=1, source_target_pairs={{0,2},{2,4},{4,6},{6,8},{8,10},{10,12},{12,14},{1,3},{3,5},{5,7},{... | collective-permute-start | bytes 589832 | tf_op jit(solution)/shard_map/ppermute | solution.py:16
  144.1 1.5 collective-permute-start.7
  145.6 3.2 %fusion.18 = bf16[256,1536]{1,0:T(8,128)(2,1)} fusion(bf16[256,1536]{1,0:T(8,128)(2,1)} %fusion.54, bf16[256,1536]{1,0:T(8,128)(2,1)} %copy-done.2, bf16[256,1536]{1,0:T(8,128)(2,1)S(1)} %collective-permute-done.5, bf16[1,1536,256]{2,1,0:T(8,128)(2,1)S(1)} %copy-done, pred[]{:T(512)S(6)} %eq.8), kind=kOutput, calls=%fused_computation.26 | convolution fusion | flops 403111936 | bytes 3932161 | tf_op jit(solution)/shard_map/dot_general | solution.py:82
  148.7 0.0 reduce-scatter.2.cloned.1.call-update
  148.8 0.0 copy-start.6
  148.8 0.0 collective-permute-done.6
  148.8 4.7 %collective-permute-done.7 = bf16[64,1536]{1,0:T(8,128)(2,1)S(1)} collective-permute-done((bf16[64,1536]{1,0:T(8,128)(2,1)}, bf16[64,1536]{1,0:T(8,128)(2,1)S(1)}, u32[]{:S(2)}, u32[]{:S(2)}) %collective-permute-start.7) | collective-permute-done | bytes 196640 | tf_op jit(solution)/shard_map/ppermute | solution.py:17
  153.5 0.1 pad_maximum_fusion.2
  153.6 2.4 %fusion.53 = (f32[256]{0:T(256)S(1)}, f32[256,1536]{1,0:T(8,128)S(1)}) fusion(bf16[1,256,1536]{2,1,0:T(8,128)(2,1)S(1)} %copy-done.1, f32[256]{0:T(256)S(1)} %copy-done.8, bf16[384,1536]{1,0:T(8,128)(2,1)S(1)} %pad_maximum_fusion.2, s32[]{:T(128)S(6)} %select_n.35, f32[1536]{0:T(1024)S(1)} %get-tuple-element.3, bf16[256,1536]{1,0:T(8,128)(2,1)S(1)} %fusion.25, ...), kind=kLoop, calls=%fused_computation.57 | loop fusion | flops 12189440 | bytes 4739080 | tf_op jit(solution)/shard_map/transpose(jvp())/reduce_sum | solution.py:29
  156.0 0.5 fusion.37
  156.5 1.3 collective-permute-start.8
  157.8 1.3 collective-permute-done.8
  159.1 0.8 fusion.67
  159.9 55.5 %reduce-scatter.2.cloned.1.call-done = bf16[32,1536]{1,0:T(8,128)(2,1)} async-done(((bf16[256,1536]{1,0:T(8,128)(2,1)}), bf16[32,1536]{1,0:T(8,128)(2,1)}) %reduce-scatter.2.cloned.1.call-update) | async-done | bytes 98320 | tf_op jit(solution)/shard_map/reduce_scatter | solution.py:101
  215.4 5.5 %all-gather = bf16[64,1536]{1,0:T(8,128)(2,1)S(1)} all-gather(bf16[32,1536]{1,0:T(8,128)(2,1)} %reduce-scatter.2.cloned.1.call-done), channel_id=2, replica_groups=mesh['dp'=2,'ctx'=8,'segment'=2] {'dp'}, dimensions={0}, use_global_device_ids=true | all-gather | bytes 294912 | tf_op jit(solution)/shard_map/all_gather | solution.py:106
  220.9 0.7 bitcast_convert_fusion
  (24 shorter events, 0.2 us)
Async XLA Ops:
  7.2 123.8 %copy-start = (bf16[1,1536,256]{2,1,0:T(8,128)(2,1)S(1)}, bf16[1,1536,256]{2,1,0:T(8,128)(2,1)}, u32[]{:S(2)}) copy-start(bf16[1,1536,256]{2,1,0:T(8,128)(2,1)} %param.10) | copy-start | bytes 2359300
  7.2 2.8 %copy-start.1 = (bf16[1,256,1536]{2,1,0:T(8,128)(2,1)S(1)}, bf16[1,256,1536]{2,1,0:T(8,128)(2,1)}, u32[]{:S(2)}) copy-start(bf16[1,256,1536]{2,1,0:T(8,128)(2,1)} %param.6) | copy-start | bytes 2359300
  7.2 85.2 %all-gather.3.cloned.1.call-start = ((), (), s32[]{:S(2)}) async-start(), calls=%async_computation.1 | async-start | bytes 5308416 | tf_op jit(solution)/shard_map/all_gather | solution.py:49
  7.9 8.9 %copy-start.12 = (s32[2]{0:T(128)S(1)}, s32[2]{0:T(128)}, u32[]{:S(2)}) copy-start(s32[2]{0:T(128)} %param.11) | copy-start | bytes 28
  7.9 10.8 %copy-start.9 = (f32[1,3,1536]{2,0,1:T(1,128)S(1)}, f32[1,3,1536]{2,0,1:T(1,128)}, u32[]{:S(2)}) copy-start(f32[1,3,1536]{2,0,1:T(1,128)} %param.9) | copy-start | bytes 55300
  7.9 207.4 %reduce-scatter.2.cloned.1.call-start = ((), (), s32[]{:S(2)}) async-start(), calls=%async_computation.2 | async-start | bytes 884736 | tf_op jit(solution)/shard_map/reduce_scatter | solution.py:101
  9.4 0.6 copy-start.10
  9.9 14.0 %copy-start.7 = (f32[256]{0:T(256)}, f32[256]{0:T(256)S(1)}, u32[]{:S(2)}) copy-start(f32[256]{0:T(256)S(1)} %fusion.69) | copy-start | bytes 3076
  10.6 9.1 %collective-permute-start.2 = (bf16[64,1536]{1,0:T(8,128)(2,1)S(1)}, bf16[64,1536]{1,0:T(8,128)(2,1)S(1)}, u32[]{:S(2)}, u32[]{:S(2)}) collective-permute-start(bf16[64,1536]{1,0:T(8,128)(2,1)S(1)} %get-tuple-element.16), channel_id=1, source_target_pairs={{0,2},{2,4},{4,6},{6,8},{8,10},{10,12},{12,14},{1,3},{3,5},{5,7},{... | collective-permute-start | bytes 589832 | tf_op jit(solution)/shard_map/ppermute | solution.py:16
  15.5 8.3 %collective-permute-start.3 = (bf16[64,1536]{1,0:T(8,128)(2,1)S(1)}, bf16[64,1536]{1,0:T(8,128)(2,1)S(1)}, u32[]{:S(2)}, u32[]{:S(2)}) collective-permute-start(bf16[64,1536]{1,0:T(8,128)(2,1)S(1)} %get-tuple-element.17), channel_id=1, source_target_pairs={{2,0},{4,2},{6,4},{8,6},{10,8},{12,10},{14,12},{3,1},{5,3},{7,5},{... | collective-permute-start | bytes 589832 | tf_op jit(solution)/shard_map/ppermute | solution.py:17
  18.8 90.6 %copy-start.5 = (f32[1536]{0:T(1024)}, f32[1536]{0:T(1024)S(1)}, u32[]{:S(2)}) copy-start(f32[1536]{0:T(1024)S(1)} %get-tuple-element.4) | copy-start | bytes 18436
  25.1 67.2 %copy-start.2 = (bf16[256,1536]{1,0:T(8,128)(2,1)}, bf16[256,1536]{1,0:T(8,128)(2,1)S(1)}, u32[]{:S(2)}) copy-start(bf16[256,1536]{1,0:T(8,128)(2,1)S(1)} %add_convert_fusion.1) | copy-start | bytes 2359300
  25.2 72.4 %copy-start.3 = (bf16[1,256,1536]{2,1,0:T(8,128)(2,1)S(1)}, bf16[1,256,1536]{2,1,0:T(8,128)(2,1)}, u32[]{:S(2)}) copy-start(bf16[1,256,1536]{2,1,0:T(8,128)(2,1)} %param.7) | copy-start | bytes 2359300
  92.4 5.2 %copy-start.13 = (bf16[1,1536,1536]{2,1,0:T(8,128)(2,1)S(1)}, bf16[1,1536,1536]{2,1,0:T(8,128)(2,1)}, u32[]{:S(2)}) copy-start(bf16[1,1536,1536]{2,1,0:T(8,128)(2,1)} %all-gather.3.cloned.1.call-done) | copy-start | bytes 14155780
  96.2 13.0 %collective-permute-start.4 = (bf16[256,1536]{1,0:T(8,128)(2,1)S(1)}, bf16[256,1536]{1,0:T(8,128)(2,1)S(1)}, u32[]{:S(2)}, u32[]{:S(2)}) collective-permute-start(bf16[256,1536]{1,0:T(8,128)(2,1)S(1)} %fusion.19), channel_id=1, source_target_pairs={{0,1},{2,3},{4,5},{6,7},{8,9},{10,11},{12,13},{14,15},{16,17},{18,... | collective-permute-start | bytes 2359304 | tf_op jit(solution)/shard_map/ppermute | solution.py:25
  99.1 7.7 %collective-permute-start = (bf16[64,1536]{1,0:T(8,128)(2,1)S(1)}, bf16[64,1536]{1,0:T(8,128)(2,1)S(1)}, u32[]{:S(2)}, u32[]{:S(2)}) collective-permute-start(bf16[64,1536]{1,0:T(8,128)(2,1)S(1)} %get-tuple-element.14), channel_id=1, source_target_pairs={{0,2},{2,4},{4,6},{6,8},{8,10},{10,12},{12,14},{1,3},{3,5},{5,7},{... | collective-permute-start | bytes 589832 | tf_op jit(solution)/shard_map/ppermute | solution.py:16
  101.5 7.6 %collective-permute-start.1 = (bf16[64,1536]{1,0:T(8,128)(2,1)S(1)}, bf16[64,1536]{1,0:T(8,128)(2,1)S(1)}, u32[]{:S(2)}, u32[]{:S(2)}) collective-permute-start(bf16[64,1536]{1,0:T(8,128)(2,1)S(1)} %get-tuple-element.15), channel_id=1, source_target_pairs={{2,0},{4,2},{6,4},{8,6},{10,8},{12,10},{14,12},{3,1},{5,3},{7,5},{... | collective-permute-start | bytes 589832 | tf_op jit(solution)/shard_map/ppermute | solution.py:17
  109.4 2.5 %copy-start.4 = (bf16[1,256,1536]{2,1,0:T(8,128)(2,1)S(1)}, bf16[1,256,1536]{2,1,0:T(8,128)(2,1)}, u32[]{:S(2)}) copy-start(bf16[1,256,1536]{2,1,0:T(8,128)(2,1)} %param.7) | copy-start | bytes 2359300
  113.3 21.5 %collective-permute-start.5 = (bf16[256,1536]{1,0:T(8,128)(2,1)}, bf16[256,1536]{1,0:T(8,128)(2,1)S(1)}, u32[]{:S(2)}, u32[]{:S(2)}) collective-permute-start(bf16[256,1536]{1,0:T(8,128)(2,1)} %fusion.35), channel_id=1, source_target_pairs={{1,0},{3,2},{5,4},{7,6},{9,8},{11,10},{13,12},{15,14},{17,16},{19,... | collective-permute-start | bytes 2359304 | tf_op jit(solution)/shard_map/ppermute | solution.py:25
  115.4 10.0 %collective-permute-start.9 = (bf16[64,1536]{1,0:T(8,128)(2,1)}, bf16[64,1536]{1,0:T(8,128)(2,1)S(1)}, u32[]{:S(2)}, u32[]{:S(2)}) collective-permute-start(bf16[64,1536]{1,0:T(8,128)(2,1)} %get-tuple-element.10), channel_id=1, source_target_pairs={{0,2},{2,4},{4,6},{6,8},{8,10},{10,12},{12,14},{1,3},{3,5},{5,7},{... | collective-permute-start | bytes 589832 | tf_op jit(solution)/shard_map/ppermute | solution.py:16
  120.0 9.8 %collective-permute-start.10 = (bf16[64,1536]{1,0:T(8,128)(2,1)}, bf16[64,1536]{1,0:T(8,128)(2,1)S(1)}, u32[]{:S(2)}, u32[]{:S(2)}) collective-permute-start(bf16[64,1536]{1,0:T(8,128)(2,1)} %get-tuple-element.11), channel_id=1, source_target_pairs={{2,0},{4,2},{6,4},{8,6},{10,8},{12,10},{14,12},{3,1},{5,3},{7,5},{... | collective-permute-start | bytes 589832 | tf_op jit(solution)/shard_map/ppermute | solution.py:17
  139.4 9.4 %collective-permute-start.6 = (bf16[64,1536]{1,0:T(8,128)(2,1)}, bf16[64,1536]{1,0:T(8,128)(2,1)S(1)}, u32[]{:S(2)}, u32[]{:S(2)}) collective-permute-start(bf16[64,1536]{1,0:T(8,128)(2,1)} %get-tuple-element.12), channel_id=1, source_target_pairs={{0,2},{2,4},{4,6},{6,8},{8,10},{10,12},{12,14},{1,3},{3,5},{5,7},{... | collective-permute-start | bytes 589832 | tf_op jit(solution)/shard_map/ppermute | solution.py:16
  144.1 9.4 %collective-permute-start.7 = (bf16[64,1536]{1,0:T(8,128)(2,1)}, bf16[64,1536]{1,0:T(8,128)(2,1)S(1)}, u32[]{:S(2)}, u32[]{:S(2)}) collective-permute-start(bf16[64,1536]{1,0:T(8,128)(2,1)} %get-tuple-element.13), channel_id=1, source_target_pairs={{2,0},{4,2},{6,4},{8,6},{10,8},{12,10},{14,12},{3,1},{5,3},{7,5},{... | collective-permute-start | bytes 589832 | tf_op jit(solution)/shard_map/ppermute | solution.py:17
  148.8 4.8 %copy-start.6 = (f32[1536]{0:T(1024)S(1)}, f32[1536]{0:T(1024)}, u32[]{:S(2)}) copy-start(f32[1536]{0:T(1024)} %copy-done.5) | copy-start | bytes 18436
  148.8 4.8 %copy-start.8 = (f32[256]{0:T(256)S(1)}, f32[256]{0:T(256)}, u32[]{:S(2)}) copy-start(f32[256]{0:T(256)} %copy-done.7) | copy-start | bytes 3076
  153.6 2.4 %copy-start.11 = (f32[256]{0:T(256)S(1)}, f32[256]{0:T(256)}, u32[]{:S(2)}) copy-start(f32[256]{0:T(256)} %copy-done.10) | copy-start | bytes 3076
  156.5 2.6 %collective-permute-start.8 = (bf16[256,768]{1,0:T(8,128)(2,1)S(1)}, bf16[256,768]{1,0:T(8,128)(2,1)S(1)}, u32[]{:S(2)}, u32[]{:S(2)}) collective-permute-start(bf16[256,768]{1,0:T(8,128)(2,1)S(1)} %slice.79), channel_id=1, source_target_pairs={{0,1},{2,3},{4,5},{6,7},{8,9},{10,11},{12,13},{14,15},{16,17},{18,... | collective-permute-start | bytes 1179656 | tf_op jit(solution)/shard_map/ppermute | solution.py:25
Sparse Core Ops, SparseCore 0:
  10.2 82.1 all-gather.2
  148.9 66.4 reduce-scatter.1
